TPU v7x, 512 devices: a whole 4x4x16 slice. The times are simulated.
512 devices in a mesh: replica: 128 (over y, z_lo, x), dp: 4 (over z_hi, core).
Axes of the slice: x: 4, y: 4, z: 16 (z_hi: 2, z_lo: 8; z = z_hi * 8 + z_lo), core: 2. Of those that a mesh axis runs over, the one named last changes fastest.
Arguments:
- block_input: bfloat16 [1024, 288, 680], P(('replica', 'dp')), may hold values from -40 to 40
- time_shift: bfloat16 [1024, 680], P(('replica', 'dp')), may hold values from -4 to 4
- out_grad: bfloat16 [1024, 288, 680], P(('replica', 'dp')), may hold values from -6 to 6
- params: float32 [128, 680, 680], P('replica', 'dp'), may hold values from -0.21875 to 0.21875
- first_moment: float32 [128, 680, 680], P('replica', 'dp'), may hold values from -8 to 8
- second_moment: float32 [128, 680, 680], P('replica', 'dp'), may hold values from 1 to 20
- push_weight: float32 [128], P('replica'), may hold values from 0.5 to 2
- step: int32 [1], replicated, may hold values from 0 to 999
Outputs:
- grad_input: bfloat16 [1024, 288, 680], P(('replica', 'dp'))
- new_params: float32 [128, 680, 680], P('replica', 'dp')
- new_first: float32 [128, 680, 680], P('replica', 'dp')
- new_second: float32 [128, 680, 680], P('replica', 'dp')
- new_weight: float32 [128], P('replica')
All inputs are finite; a program needn't handle non-finite values.
Results may differ from a plain program's by a relative error of at most 0.006.
Values may be sent and summed in bfloat16 or wider, within the bound.
A program may use at most 64 MiB of HBM per device.

v0:
```python
import functools

import jax
import jax.numpy as jnp
from jax import lax
from jax.experimental import pallas as pl
from jax.experimental.pallas import tpu as pltpu
from jax.sharding import PartitionSpec as P

MESH = pl.DeviceIdType.MESH
F32 = jnp.float32
BF16 = jnp.bfloat16
HIGHEST = lax.Precision.HIGHEST

GSIZE = 40
NORM_EPS = 1e-05
BETA_ONE = 0.9
BETA_TWO = 0.999
LEARN_RATE = 0.002
ADAM_EPS = 1e-08

LANES = 128
USED = 120
REST = 64
SLOT = 176


def iota(shape, dim):
    return lax.broadcasted_iota(jnp.int32, shape, dim)


def dot(a, b, **kw):
    return jnp.dot(a, b, preferred_element_type=F32, **kw)


def dot_nt(a, b):
    return lax.dot_general(a, b, (((1,), (1,)), ((), ())), preferred_element_type=F32)


def sigmoid(v):
    return 0.5 * jnp.tanh(0.5 * v) + 0.5


def pack_rest(last):
    lane = iota((REST, LANES), 1)
    third = jnp.concatenate(
        [last[2 * REST :], jnp.zeros((3 * REST - SLOT, LANES), last.dtype)], axis=0
    )
    second = pltpu.roll(last[REST : 2 * REST], GSIZE, 1)
    third = pltpu.roll(third, 2 * GSIZE, 1)
    return jnp.where(lane < GSIZE, last[:REST], jnp.where(lane < 2 * GSIZE, second, third))


def unpack_rest(packed):
    second = pltpu.roll(packed, LANES - GSIZE, 1)
    third = pltpu.roll(packed, LANES - 2 * GSIZE, 1)
    whole = jnp.concatenate([packed, second, third[: SLOT - 2 * REST]], axis=0)
    return jnp.where(iota((SLOT, LANES), 1) < GSIZE, whole, 0.0)


def step_kernel(
    x_hbm, shift_ref, og_hbm, par_hbm, mom_hbm, sec_hbm, push_ref, step_ref,
    gi_ref, moved_ref, first_ref, second_ref, gsend,
    x_ref, og_ref, par_ref, mom_ref, sec_ref,
    nat, wall, wnat, wgrp, act, act_t, xn, dsil, ogg, tsg, gh, dw, dwn, dw_in, own, bsend, brecv,
    load,
    a_core_s, a_core_r, a_z_s, a_z_r, a_rel_s, a_rel_r, b_core_s, b_core_r, b_z_s, b_z_r,
):
    samples, positions, channels = x_ref.shape
    rows = par_ref.shape[0]
    tiles = wgrp.shape[0]
    last = tiles - 1
    replica, dp = lax.axis_index("replica"), lax.axis_index("dp")
    far, core = dp // 2, lax.rem(dp, 2)
    partner = (replica, far * 2 + 1 - core)
    across = (replica, (1 - far) * 2 + core)
    mine, across_slot = core * 2 + far, core * 2 + 1 - far

    loads = [
        pltpu.make_async_copy(source, target, load.at[n])
        for n, (source, target) in enumerate(
            (
                (par_hbm.at[:, 0, :], par_ref),
                (x_hbm, x_ref),
                (og_hbm, og_ref),
                (mom_hbm.at[:, 0, :], mom_ref),
                (sec_hbm.at[:, 0, :], sec_ref),
            )
        )
    ]
    for copy in loads:
        copy.start()

    barrier = pltpu.get_barrier_semaphore()
    for peer in (partner, across):
        pl.semaphore_signal(barrier, inc=1, device_id=peer, device_id_type=MESH)

    def remote(src, dst, s, r, to):
        return pltpu.make_async_remote_copy(
            src_ref=src, dst_ref=dst, send_sem=s, recv_sem=r, device_id=to, device_id_type=MESH
        )

    def part(ref, rest):
        return ref.at[pl.ds(0, REST)] if rest else ref

    def a_core(t, rest=False):
        block = part(wall.at[t, mine], rest)
        return remote(block, block, a_core_s.at[t], a_core_r.at[t], partner)

    def a_z(t, rest=False):
        block = part(wall.at[t, mine], rest)
        return remote(block, block, a_z_s.at[t], a_z_r.at[t], across)

    def a_rel(t, rest=False):
        block = part(wall.at[t, across_slot], rest)
        return remote(block, block, a_rel_s.at[t], a_rel_r.at[t], partner)

    def b_core(t):
        return remote(dwn.at[t, 1 - core], dw_in.at[t], b_core_s.at[t], b_core_r.at[t], partner)

    def b_z(t, rest=False):
        return remote(
            part(bsend.at[t], rest), part(brecv.at[t], rest), b_z_s.at[t], b_z_r.at[t], across
        )

    lane = iota((SLOT, LANES), 1)

    nat[SLOT - 8 : SLOT, :] = jnp.zeros((8, nat.shape[1]), F32)
    nat[:, last * LANES :] = jnp.zeros((SLOT, LANES), F32)
    loads[0].wait()
    nat[0:rows, 0:channels] = par_ref[...] / push_ref[0]
    pl.semaphore_wait(barrier, 2)
    for t in range(last):
        wall[t, mine] = nat[:, t * LANES : (t + 1) * LANES].astype(BF16)
        a_z(t).start()
        a_core(t).start()
    wall[last, mine, 0:REST] = pack_rest(nat[:, last * LANES :]).astype(BF16)
    a_z(last, True).start()
    a_core(last, True).start()

    def group_of(index):
        total = jnp.zeros_like(index)
        for g in range(1, channels // GSIZE):
            total = total + (index >= g * GSIZE).astype(jnp.int32)
        return total

    to_group = (group_of(iota((channels, LANES), 0)) == iota((channels, LANES), 1)).astype(F32)
    from_group = (iota((LANES, channels), 0) == group_of(iota((LANES, channels), 1))).astype(F32)

    def stack(totals, width):
        row = iota((8, width), 0)
        out = jnp.zeros((8, width), F32)
        for n, total in enumerate(totals):
            out = jnp.where(row == n, total, out)
        return out

    def spread(totals):
        total = stack(totals, channels)
        return dot(dot(total, to_group, precision=HIGHEST), from_group, precision=HIGHEST) / entries

    def column_sum(values):
        return jnp.sum(values, axis=0, keepdims=True)

    entries = positions * GSIZE
    spans = [pl.ds(s * positions, positions) for s in range(samples)]

    loads[1].wait()
    average = spread([column_sum(x_ref[s].astype(F32)) for s in range(samples)])
    squares = []
    for s in range(samples):
        centered = x_ref[s].astype(F32) - average[s : s + 1]
        xn[spans[s], :] = centered
        squares.append(column_sum(centered * centered))
    inverse_in = lax.rsqrt(spread(squares) + NORM_EPS)
    for s in range(samples):
        normed = xn[spans[s], :] * inverse_in[s : s + 1]
        sig = sigmoid(normed)
        xn[spans[s], :] = normed
        act[spans[s], :] = (normed * sig).astype(BF16)
        dsil[spans[s], :] = sig * (1.0 + normed * (1.0 - sig))

    def source_of(index):
        out = index
        for q, owner in enumerate((0, 2, 1, 3)):
            inside = (index >= q * SLOT) & (index < q * SLOT + rows)
            shifted = index - q * SLOT + owner * rows
            out = jnp.where(inside, shifted, out)
            out = jnp.where((index >= q * SLOT + rows) & (index < (q + 1) * SLOT), -1, out)
        return out

    padded = 4 * SLOT
    unpad = (iota((channels, padded), 0) == source_of(iota((channels, padded), 1))).astype(BF16)
    pad = (source_of(iota((padded, channels), 0)) == iota((padded, channels), 1)).astype(BF16)
    act_t[...] = dot_nt(pad, act[...]).astype(BF16)

    shifts = jnp.concatenate(
        [shift_ref[...].astype(F32), jnp.zeros((16 - samples, channels), F32)], axis=0
    ).astype(BF16)

    loads[2].wait()

    def regroup(t, _):
        column = iota((channels, LANES), 1)
        select = (iota((channels, LANES), 0) == column + t * USED) & (column < USED)
        select = select.astype(F32).astype(BF16)
        for s in range(samples):
            ogg[t, spans[s], :] = dot(og_ref[s], select).astype(BF16)
        tsg[t] = dot(shifts, select)
        return 0

    lax.fori_loop(0, tiles, regroup, 0)

    lane8 = iota((8, LANES), 1)

    def tile_spread(totals):
        total = stack(totals, LANES) / entries
        sums = [
            jnp.sum(
                jnp.where((lane8 >= g * GSIZE) & (lane8 < (g + 1) * GSIZE), total, 0.0),
                axis=1,
                keepdims=True,
            )
            for g in range(3)
        ]
        return jnp.where(
            lane8 < GSIZE,
            sums[0],
            jnp.where(lane8 < 2 * GSIZE, sums[1], jnp.where(lane8 < USED, sums[2], 0.0)),
        )

    def to_natural(t, this, after):
        wide = this.shape
        column = iota(wide, 1)
        this = pltpu.roll(this, lax.rem(LANES - 8 * t, LANES), 1)
        after = pltpu.roll(after, USED - 8 * t, 1)
        return jnp.where(column < USED - 8 * t, this, after)

    def exchange(t, this, after):
        dwn[t] = to_natural(t, this, after).reshape(2, 2, SLOT, LANES)
        b_core(t).start()

    def finish(t, rest=False):
        b_core(t).wait_recv()
        away = dwn[t, core, 1 - far] + dw_in[t, 1 - far]
        if rest:
            bsend[t, 0:REST] = pack_rest(away).astype(BF16)
        else:
            bsend[t] = away.astype(BF16)
        b_z(t, rest).start()
        own[t] = dwn[t, core, far] + dw_in[t, far]

    def relay(t, rest=False):
        a_z(t, rest).wait_recv()
        a_rel(t, rest).start()

    relay(0)

    def tile_step(t, _):
        @pl.when(t + 1 < last)
        def _():
            relay(t + 1)

        @pl.when(t + 1 == last)
        def _():
            relay(last, True)

        @pl.when(t < last)
        def _():
            a_core(t).wait_recv()
            a_rel(t).wait_recv()

        @pl.when(t == last)
        def _():
            a_core(last, True).wait_recv()
            a_rel(last, True).wait_recv()
            for q in range(4):
                wall[tiles, q] = unpack_rest(wall[last, q, 0:REST].astype(F32)).astype(BF16)

        wide = (channels, LANES)
        column = iota(wide, 1)
        this = dot(unpad, wall[t + t // last].reshape(padded, LANES))
        wnat[lax.rem(t, 2)] = this
        before = wnat[lax.rem(t + 1, 2)]
        weight = jnp.where(
            column < 8 * t, pltpu.roll(before, 8 * t, 1), pltpu.roll(this, 8 * t, 1)
        )
        weight = jnp.where(column < USED, weight, 0.0).astype(BF16)
        wgrp[t] = weight

        hidden = [dot(act[span, :], weight) + tsg[t, s : s + 1, :] for s, span in enumerate(spans)]
        average = tile_spread([column_sum(h) for h in hidden])
        hidden = [h - average[s : s + 1] for s, h in enumerate(hidden)]
        variance = tile_spread([column_sum(h * h) for h in hidden])
        inverse = lax.rsqrt(variance + NORM_EPS)
        normed = [h * inverse[s : s + 1] for s, h in enumerate(hidden)]
        grads = []
        for s, n in enumerate(normed):
            sig = sigmoid(n)
            grads.append(ogg[t, spans[s], :].astype(F32) * (sig * (1.0 + n * (1.0 - sig))))
        means = tile_spread(
            [column_sum(g) for g in grads] + [column_sum(g * n) for g, n in zip(grads, normed)]
        )
        for s, (g, n) in enumerate(zip(grads, normed)):
            one, two = means[s : s + 1], means[samples + s : samples + s + 1]
            gh[t, spans[s], :] = (inverse[s : s + 1] * (g - one - n * two)).astype(BF16)

        now = lax.rem(t, 2)
        dw[now] = dot(act_t[...], gh[t])

        @pl.when(t > 0)
        def _():
            exchange(t - 1, dw[1 - now], dw[now])

        @pl.when(t > 1)
        def _():
            finish(t - 2)

        return 0

    wnat[1] = jnp.zeros((channels, LANES), F32)
    lax.fori_loop(0, tiles, tile_step, 0)
    exchange(last, dw[last % 2], dw[last % 2])
    finish(last - 1)

    sums_one, sums_two = [], []
    for s, span in enumerate(spans):
        total = jnp.zeros((positions, channels), F32)
        for t in range(tiles):
            total = total + dot_nt(gh[t, span, :], wgrp[t])
        grad_val = total * dsil[span, :]
        dsil[span, :] = grad_val
        sums_one.append(column_sum(grad_val))
        sums_two.append(column_sum(grad_val * xn[span, :]))
        if s == 0:
            finish(last, True)
    means = spread(sums_one + sums_two)
    for s, span in enumerate(spans):
        one, two = means[s : s + 1], means[samples + s : samples + s + 1]
        grad_val = dsil[span, :] - one - xn[span, :] * two
        gi_ref[s] = (inverse_in[s : s + 1] * grad_val).astype(BF16)

    count = jnp.full((1, LANES), (step_ref[0] + 1).astype(F32))
    fix_one = 1.0 - jnp.power(jnp.full((1, LANES), BETA_ONE, F32), count)
    fix_two = 1.0 - jnp.power(jnp.full((1, LANES), BETA_TWO, F32), count)
    loads[3].wait()
    loads[4].wait()
    extra = jnp.full((SLOT - rows, LANES), push_ref[0], F32)

    for t in range(tiles):
        rest = t == last
        width = min(LANES, channels - t * LANES)
        cols = pl.ds(t * LANES, width)
        b_z(t, rest).wait_recv()
        if rest:
            arrived = unpack_rest(brecv[t, 0:REST].astype(F32))
        else:
            arrived = brecv[t].astype(F32)
        grad = (0.25 * (own[t] + arrived))[0:rows, 0:width]
        first_new = BETA_ONE * mom_ref[:, cols] + (1.0 - BETA_ONE) * grad
        second_new = BETA_TWO * sec_ref[:, cols] + (1.0 - BETA_TWO) * grad * grad
        first_ref[:, cols] = first_new
        second_ref[:, cols] = second_new
        update = LEARN_RATE * (first_new / fix_one[:, 0:width])
        update = update / (jnp.sqrt(second_new / fix_two[:, 0:width]) + ADAM_EPS)
        moved = par_ref[:, cols] - update
        moved_ref[:, cols] = moved
        nat[0:rows, cols] = moved
        nat[rows:SLOT, t * LANES : (t + 1) * LANES] = extra
        moved = nat[:, t * LANES : (t + 1) * LANES]
        if rest:
            gsend[t, 0:REST] = pack_rest(moved).astype(BF16)
            gsend[t, REST:] = jnp.zeros((SLOT - REST, LANES), BF16)
        else:
            gsend[t] = moved.astype(BF16)

    for t in range(tiles):
        rest = t == last
        for copy in (a_core(t, rest), a_z(t, rest), a_rel(t, rest), b_z(t, rest)):
            copy.wait_send()
        b_core(t).wait_send()


def gossip_kernel(distance, send, arrived, send_sem, recv_sem):
    replica, dp = lax.axis_index("replica"), lax.axis_index("dp")
    replicas = lax.axis_size("replica")
    ahead = (lax.rem(replica + distance, replicas), dp)
    behind = (lax.rem(replica + replicas - distance, replicas), dp)
    barrier = pltpu.get_barrier_semaphore()
    pl.semaphore_signal(barrier, inc=1, device_id=behind, device_id_type=MESH)
    pl.semaphore_wait(barrier, 1)
    copy = pltpu.make_async_remote_copy(
        src_ref=send, dst_ref=arrived, send_sem=send_sem, recv_sem=recv_sem,
        device_id=ahead, device_id_type=MESH,
    )
    copy.start()
    copy.wait()


def gossip(distance, number, tiles):
    vmem = pl.BlockSpec(memory_space=pltpu.VMEM)
    return pl.pallas_call(
        functools.partial(gossip_kernel, distance),
        out_shape=jax.ShapeDtypeStruct(tiles.shape, BF16),
        in_specs=[vmem],
        out_specs=vmem,
        scratch_shapes=[pltpu.SemaphoreType.DMA, pltpu.SemaphoreType.DMA],
        compiler_params=pltpu.CompilerParams(
            collective_id=number, has_side_effects=True, vmem_limit_bytes=4 << 20
        ),
    )(tiles)


def output_kernel(
    gi_in, moved, first_in, second_in, near, push,
    gi_out, params_out, first_out, second_out, weight_out,
    average, sem,
):
    rows, channels = moved.shape
    tiles, last = near.shape[0], near.shape[0] - 1
    copies = [
        pltpu.make_async_copy(gi_in, gi_out, sem.at[0]),
        pltpu.make_async_copy(first_in, first_out.at[:, 0, :], sem.at[1]),
        pltpu.make_async_copy(second_in, second_out.at[:, 0, :], sem.at[2]),
        pltpu.make_async_copy(average, params_out.at[:, 0, :], sem.at[3]),
    ]
    for copy in copies[:3]:
        copy.start()
    for t in range(tiles):
        cols = pl.ds(t * LANES, min(LANES, channels - t * LANES))
        if t == last:
            arrived = unpack_rest(near[t, 0:REST].astype(F32))
        else:
            arrived = near[t].astype(F32)
        average[:, cols] = 0.5 * (moved[:, cols] + arrived[0:rows, 0 : cols.size])
        if t == 0:
            weight_out[...] = 0.5 * (push[0] + arrived[rows : rows + 1, :])
    copies[3].start()
    for copy in copies:
        copy.wait()


def write_out(grad_input, moved, first, second, near, push):
    rows, channels = moved.shape
    vmem = pl.BlockSpec(memory_space=pltpu.VMEM)
    hbm = pl.BlockSpec(memory_space=pltpu.HBM)
    square = jax.ShapeDtypeStruct((rows, 1, channels), F32)
    return pl.pallas_call(
        output_kernel,
        out_shape=(
            jax.ShapeDtypeStruct(grad_input.shape, BF16),
            square,
            square,
            square,
            jax.ShapeDtypeStruct((1, LANES), F32),
        ),
        in_specs=[vmem] * 5 + [pl.BlockSpec(memory_space=pltpu.SMEM)],
        out_specs=(hbm, hbm, hbm, hbm, vmem),
        scratch_shapes=[pltpu.VMEM((rows, channels), F32), pltpu.SemaphoreType.DMA((4,))],
        compiler_params=pltpu.CompilerParams(vmem_limit_bytes=16 << 20),
    )(grad_input, moved, first, second, near, push)


def pin(array):
    return pltpu.with_memory_space_constraint(array, pltpu.HBM)


def exchange_and_step(number, x, shift, out_grad, params, first, second, push, step):
    samples, positions, channels = x.shape
    rows = params.shape[0]
    tokens = samples * positions
    tiles = -(-channels // USED)
    vmem = pl.BlockSpec(memory_space=pltpu.VMEM)
    smem = pl.BlockSpec(memory_space=pltpu.SMEM)
    hbm = pl.BlockSpec(memory_space=pltpu.HBM)
    dma = pltpu.SemaphoreType.DMA((tiles,))
    square = jax.ShapeDtypeStruct((rows, channels), F32)
    tile = (SLOT, LANES)
    return pl.pallas_call(
        step_kernel,
        out_shape=(
            jax.ShapeDtypeStruct(x.shape, BF16),
            square,
            square,
            square,
            jax.ShapeDtypeStruct((tiles, *tile), BF16),
        ),
        in_specs=[hbm, vmem, hbm, hbm, hbm, hbm, smem, smem],
        out_specs=(vmem,) * 5,
        scratch_shapes=[
            pltpu.VMEM(x.shape, BF16),
            pltpu.VMEM(x.shape, BF16),
        ]
        + [pltpu.VMEM((rows, channels), F32)] * 3
        + [
            pltpu.VMEM((SLOT, tiles * LANES), F32),
            pltpu.VMEM((tiles + 1, 4, *tile), BF16),
            pltpu.VMEM((2, channels, LANES), F32),
            pltpu.VMEM((tiles, channels, LANES), BF16),
            pltpu.VMEM((tokens, channels), BF16),
            pltpu.VMEM((4 * SLOT, tokens), BF16),
            pltpu.VMEM((tokens, channels), F32),
            pltpu.VMEM((tokens, channels), F32),
            pltpu.VMEM((tiles, tokens, LANES), BF16),
            pltpu.VMEM((tiles, 16, LANES), F32),
            pltpu.VMEM((tiles, tokens, LANES), BF16),
            pltpu.VMEM((2, 4 * SLOT, LANES), F32),
            pltpu.VMEM((tiles, 2, 2, *tile), F32),
            pltpu.VMEM((tiles, 2, *tile), F32),
            pltpu.VMEM((tiles, *tile), F32),
        ]
        + [pltpu.VMEM((tiles, *tile), BF16)] * 2
        + [pltpu.SemaphoreType.DMA((5,))]
        + [dma] * 10,
        compiler_params=pltpu.CompilerParams(
            collective_id=number, has_side_effects=True, vmem_limit_bytes=40 << 20
        ),
    )(pin(x), shift, pin(out_grad), pin(params), pin(first), pin(second), push, step)


def local(
    block_input, time_shift, out_grad, params, first_moment, second_moment, push_weight, step
):
    def by_row(state):
        return jnp.transpose(state, (1, 0, 2))

    level_count = lax.axis_size("replica").bit_length() - 1
    grad_input, moved, first_new, second_new, tiles = exchange_and_step(
        level_count, block_input, time_shift, out_grad, by_row(params), by_row(first_moment),
        by_row(second_moment), push_weight, step,
    )
    branches = [functools.partial(gossip, 1 << power, power) for power in range(level_count)]
    near = lax.switch(step[0] % level_count, branches, tiles)
    grad_input, averaged, first_new, second_new, new_weight = write_out(
        grad_input, moved, first_new, second_new, near, push_weight
    )
    return (
        grad_input, by_row(averaged), by_row(first_new), by_row(second_new), new_weight[0, :1]
    )


def solution(mesh):
    placed = (
        P(("replica", "dp"), None, None),
        P(("replica", "dp"), None),
        P(("replica", "dp"), None, None),
        P("replica", "dp", None),
        P("replica", "dp", None),
        P("replica", "dp", None),
        P("replica"),
        P(),
    )
    return jax.shard_map(
        local,
        mesh=mesh,
        in_specs=placed,
        out_specs=(
            P(("replica", "dp"), None, None),
            P("replica", "dp", None),
            P("replica", "dp", None),
            P("replica", "dp", None),
            P("replica"),
        ),
        check_vma=False,
    )
```

profile of v0, /device:TPU:1, one launch (start us, length us, event | category | flops | bytes accessed | tf_op | source)
XLA Modules:
  0.0 81.7 jit_solution(5743276245795482152)
XLA Ops:
  1.9 0.0 copy-start
  2.0 0.7 copy-done
  2.6 49.0 %shard_map.119 = (bf16[2,288,680]{2,1,0:T(8,128)(2,1)S(1)}, f32[170,680]{1,0:T(8,128)S(1)}, f32[170,680]{1,0:T(8,128)S(1)}, f32[170,680]{1,0:T(8,128)S(1)}, bf16[6,176,128]{2,1,0:T(8,128)(2,1)S(1)}) custom-call(bf16[2,288,680]{2,1,0:T(8,128)(2,1)} %x_hbm.1, bf16[2,680]{1,0:T(2,128)(2,1)S(1)} %copy-done, bf16[2,288,680]{2,1,0:T(8,128)(2,1)} %og_hbm.1, ...), custom_call_target="tpu_custom_call" | custom-call | tf_op jit(solution)/shard_map/pallas_call | solution.py:478
  51.7 28.1 %conditional.1 = (bf16[6,176,128]{2,1,0:T(8,128)(2,1)S(1)}) conditional(s32[]{:T(128)} %clamp.3, bf16[6,176,128]{2,1,0:T(8,128)(2,1)S(1)} %get-tuple-element.34, bf16[6,176,128]{2,1,0:T(8,128)(2,1)S(1)} %get-tuple-element.34, bf16[6,176,128]{2,1,0:T(8,128)(2,1)S(1)} %get-tuple-element.34, ...), branch_computations={%region_0.1_spmd, %region_1.2_spmd, %region_2.3_spmd, %region_3.4_... | conditional | bytes 8 | solution.py:532
  51.7 28.1 %branch_0_fun.1 = bf16[6,176,128]{2,1,0:T(8,128)(2,1)S(1)} custom-call(bf16[6,176,128]{2,1,0:T(8,128)(2,1)S(1)} %send), custom_call_target="tpu_custom_call" | custom-call | tf_op jit(solution)/shard_map/cond/branch_0_fun/pallas_call | solution.py:401
  79.8 2.0 %shard_map.120 = (bf16[2,288,680]{2,1,0:T(8,128)(2,1)}, f32[170,1,680]{2,1,0:T(1,128)}, f32[170,1,680]{2,1,0:T(1,128)}, f32[170,1,680]{2,1,0:T(1,128)}, f32[1,128]{1,0:T(1,128)}) custom-call(bf16[2,288,680]{2,1,0:T(8,128)(2,1)S(1)} %get-tuple-element.30.gi_in, f32[170,680]{1,0:T(8,128)S(1)} %get-tuple-element.31.moved, ...), custom_call_target="tpu_custom_call" | custom-call | tf_op jit(solution)/shard_map/pallas_call | solution.py:447
Async XLA Ops:
  1.9 0.7 copy-start
where the time goes:
time: 81.4 us; the launch traced here: 81.7 us
  Pallas kernels  79.1 us (97%)
  between operations  1.97 us (2%)
    pallas_call x1, Pallas kernels, exchange_and_step(): pl.pallas_call(step_kernel, out_shape=(jax.ShapeDtypeStruct(x.shape, BF16...  49 us
    pallas_call x1, Pallas kernels, gossip(): pl.pallas_call(functools.partial(gossip_kernel, distance), out_shape=jax....  28.1 us
    pallas_call x1, Pallas kernels, write_out(): pl.pallas_call(output_kernel, out_shape=(jax.ShapeDtypeStruct(grad_input....  1.97 us

commit v1 on v0

--- a/solution.py
+++ b/solution.py
@@ -59,9 +59,9 @@
 
 
 def step_kernel(
-    x_hbm, shift_ref, og_hbm, par_hbm, mom_hbm, sec_hbm, push_ref, step_ref,
+    x_hbm, shift_hbm, og_hbm, par_hbm, mom_hbm, sec_hbm, push_ref, step_ref,
     gi_ref, moved_ref, first_ref, second_ref, gsend,
-    x_ref, og_ref, par_ref, mom_ref, sec_ref,
+    x_ref, shift_ref, og_ref, par_ref, mom_ref, sec_ref,
     nat, wall, wnat, wgrp, act, act_t, xn, dsil, ogg, tsg, gh, dw, dwn, dw_in, own, bsend, brecv,
     load,
     a_core_s, a_core_r, a_z_s, a_z_r, a_rel_s, a_rel_r, b_core_s, b_core_r, b_z_s, b_z_r,
@@ -85,6 +85,7 @@
                 (og_hbm, og_ref),
                 (mom_hbm.at[:, 0, :], mom_ref),
                 (sec_hbm.at[:, 0, :], sec_ref),
+                (shift_hbm, shift_ref),
             )
         )
     ]
@@ -193,6 +194,7 @@
     pad = (source_of(iota((padded, channels), 0)) == iota((padded, channels), 1)).astype(BF16)
     act_t[...] = dot_nt(pad, act[...]).astype(BF16)
 
+    loads[5].wait()
     shifts = jnp.concatenate(
         [shift_ref[...].astype(F32), jnp.zeros((16 - samples, channels), F32)], axis=0
     ).astype(BF16)
@@ -369,14 +371,13 @@
         moved = nat[:, t * LANES : (t + 1) * LANES]
         if rest:
             gsend[t, 0:REST] = pack_rest(moved).astype(BF16)
-            gsend[t, REST:] = jnp.zeros((SLOT - REST, LANES), BF16)
         else:
             gsend[t] = moved.astype(BF16)
 
     for t in range(tiles):
         rest = t == last
-        for copy in (a_core(t, rest), a_z(t, rest), a_rel(t, rest), b_z(t, rest)):
-            copy.wait_send()
+        for copy in (a_core, a_z, a_rel, b_z):
+            copy(t, rest).wait_send()
         b_core(t).wait_send()
 
 
@@ -388,12 +389,23 @@
     barrier = pltpu.get_barrier_semaphore()
     pl.semaphore_signal(barrier, inc=1, device_id=behind, device_id_type=MESH)
     pl.semaphore_wait(barrier, 1)
-    copy = pltpu.make_async_remote_copy(
-        src_ref=send, dst_ref=arrived, send_sem=send_sem, recv_sem=recv_sem,
-        device_id=ahead, device_id_type=MESH,
-    )
-    copy.start()
-    copy.wait()
+    last = send.shape[0] - 1
+    copies = [
+        pltpu.make_async_remote_copy(
+            src_ref=source, dst_ref=target, send_sem=send_sem.at[n], recv_sem=recv_sem.at[n],
+            device_id=ahead, device_id_type=MESH,
+        )
+        for n, (source, target) in enumerate(
+            (
+                (send.at[pl.ds(0, last)], arrived.at[pl.ds(0, last)]),
+                (send.at[last, pl.ds(0, REST)], arrived.at[last, pl.ds(0, REST)]),
+            )
+        )
+    ]
+    for copy in copies:
+        copy.start()
+    for copy in copies:
+        copy.wait()
 
 
 def gossip(distance, number, tiles):
@@ -403,7 +415,7 @@
         out_shape=jax.ShapeDtypeStruct(tiles.shape, BF16),
         in_specs=[vmem],
         out_specs=vmem,
-        scratch_shapes=[pltpu.SemaphoreType.DMA, pltpu.SemaphoreType.DMA],
+        scratch_shapes=[pltpu.SemaphoreType.DMA((2,))] * 2,
         compiler_params=pltpu.CompilerParams(
             collective_id=number, has_side_effects=True, vmem_limit_bytes=4 << 20
         ),
@@ -484,10 +496,11 @@
             square,
             jax.ShapeDtypeStruct((tiles, *tile), BF16),
         ),
-        in_specs=[hbm, vmem, hbm, hbm, hbm, hbm, smem, smem],
+        in_specs=[hbm] * 6 + [smem] * 2,
         out_specs=(vmem,) * 5,
         scratch_shapes=[
             pltpu.VMEM(x.shape, BF16),
+            pltpu.VMEM(shift.shape, BF16),
             pltpu.VMEM(x.shape, BF16),
         ]
         + [pltpu.VMEM((rows, channels), F32)] * 3
@@ -509,12 +522,12 @@
             pltpu.VMEM((tiles, *tile), F32),
         ]
         + [pltpu.VMEM((tiles, *tile), BF16)] * 2
-        + [pltpu.SemaphoreType.DMA((5,))]
+        + [pltpu.SemaphoreType.DMA((6,))]
         + [dma] * 10,
         compiler_params=pltpu.CompilerParams(
             collective_id=number, has_side_effects=True, vmem_limit_bytes=40 << 20
         ),
-    )(pin(x), shift, pin(out_grad), pin(params), pin(first), pin(second), push, step)
+    )(pin(x), pin(shift), pin(out_grad), pin(params), pin(first), pin(second), push, step)
 
 
 def local(

time: 81.4 us -> 95.2 us (1.17)
  Pallas kernels: 79.1 us -> 93 us
    pallas_call x1, Pallas kernels: 28.1 us -> 42 us  [gossip(): pl.pallas_call(functools.partial(gossip_kernel, distance), out_shape=jax....]
where the time goes in v1:
time: 95.2 us; the launch traced here: 95 us
  Pallas kernels  93 us (98%)
  between operations  1.96 us (2%)
    pallas_call x1, Pallas kernels, exchange_and_step(): pl.pallas_call(step_kernel, out_shape=(jax.ShapeDtypeStruct(x.shape, BF16...  49 us
    pallas_call x1, Pallas kernels, gossip(): pl.pallas_call(functools.partial(gossip_kernel, distance), out_shape=jax....  42 us
    pallas_call x1, Pallas kernels, write_out(): pl.pallas_call(output_kernel, out_shape=(jax.ShapeDtypeStruct(grad_input....  1.97 us

profile of v1, /device:TPU:1, one launch (start us, length us, event | category | flops | bytes accessed | tf_op | source)
XLA Modules:
  0.0 95.0 jit_solution(14125308715402726019)
XLA Ops:
  1.9 49.0 %shard_map.119 = (bf16[2,288,680]{2,1,0:T(8,128)(2,1)S(1)}, f32[170,680]{1,0:T(8,128)S(1)}, f32[170,680]{1,0:T(8,128)S(1)}, f32[170,680]{1,0:T(8,128)S(1)}, bf16[6,176,128]{2,1,0:T(8,128)(2,1)S(1)}) custom-call(bf16[2,288,680]{2,1,0:T(8,128)(2,1)} %x_hbm.1, bf16[2,680]{1,0:T(2,128)(2,1)} %shift_hbm.1, bf16[2,288,680]{2,1,0:T(8,128)(2,1)} %og_hbm.1, ...), custom_call_target="tpu_custom_call" | custom-call | tf_op jit(solution)/shard_map/pallas_call | solution.py:490
  51.0 42.1 %conditional.1 = (bf16[6,176,128]{2,1,0:T(8,128)(2,1)S(1)}) conditional(s32[]{:T(128)} %clamp.3, bf16[6,176,128]{2,1,0:T(8,128)(2,1)S(1)} %get-tuple-element.34, bf16[6,176,128]{2,1,0:T(8,128)(2,1)S(1)} %get-tuple-element.34, bf16[6,176,128]{2,1,0:T(8,128)(2,1)S(1)} %get-tuple-element.34, ...), branch_computations={%region_0.1_spmd, %region_1.2_spmd, %region_2.3_spmd, %region_3.4_... | conditional | bytes 8 | solution.py:545
  51.0 42.0 %branch_4_fun.1 = bf16[6,176,128]{2,1,0:T(8,128)(2,1)S(1)} custom-call(bf16[6,176,128]{2,1,0:T(8,128)(2,1)S(1)} %send.4), custom_call_target="tpu_custom_call" | custom-call | tf_op jit(solution)/shard_map/cond/branch_4_fun/pallas_call | solution.py:413
  93.1 2.0 %shard_map.120 = (bf16[2,288,680]{2,1,0:T(8,128)(2,1)}, f32[170,1,680]{2,1,0:T(1,128)}, f32[170,1,680]{2,1,0:T(1,128)}, f32[170,1,680]{2,1,0:T(1,128)}, f32[1,128]{1,0:T(1,128)}) custom-call(bf16[2,288,680]{2,1,0:T(8,128)(2,1)S(1)} %get-tuple-element.30.gi_in, f32[170,680]{1,0:T(8,128)S(1)} %get-tuple-element.31.moved, ...), custom_call_target="tpu_custom_call" | custom-call | tf_op jit(solution)/shard_map/pallas_call | solution.py:459
